TPU v7x, 32 devices: a whole 2x2x4 slice. The times are simulated.
32 devices in a mesh: pair: 8 (over y, x, core), idx: 4 (over z).
Axes of the slice: x: 2, y: 2, z: 4, core: 2. Of those that a mesh axis runs over, the one named last changes fastest.
Arguments:
- g2: bfloat16 [512, 512, 2, 1, 512], P('pair', None, None, None, 'idx'), may hold values from -6 to 6
- core_ham: float32 [512, 512], replicated, may hold values from -0.25 to 0.25
- dipole: float32 [512, 512], replicated, may hold values from -0.125 to 0.125
- field: float32 [1], replicated, may hold values from 0.5 to 1.5
- rho: bfloat16 [2, 512, 512], replicated, may hold values from -6 to 6
- factors: bfloat16 [2048, 512, 512], P(None, 'pair', 'idx'), may hold values from -0.046875 to 0.046875
- damping: float32 [512], replicated, may hold values from 0.02 to 0.2
Outputs:
- g2_next: bfloat16 [512, 512, 2, 1, 512], P('pair', None, None, None, 'idx')
All inputs are finite; a program needn't handle non-finite values.
Results may differ from a plain program's by a relative error of at most 0.0056.
Values may be sent and summed in bfloat16 or wider, within the bound.
A program may use at most 384 MiB of HBM per device.

v0:
```python
import jax
import jax.numpy as jnp
from jax import lax
from jax.sharding import PartitionSpec as P


def combine(total_x, total_z, rho_part):
    real = (
        total_z[:, 0, None, None] * rho_part[0][None]
        - total_z[:, 1, None, None] * rho_part[1][None]
    )
    imag = (
        total_z[:, 0, None, None] * rho_part[1][None]
        + total_z[:, 1, None, None] * rho_part[0][None]
    )
    return total_x + jnp.stack([real, imag], axis=1)


def per_device(g2, core_ham, dipole, field, rho, factors, damping):
    step_size = 1.0
    rows_loc, width, _, slab, cols_loc = g2.shape
    rank = factors.shape[0]
    kcols = factors.shape[2]
    pair_pos = lax.axis_index("pair")
    idx_pos = lax.axis_index("idx")
    hamil = 0.5 * (core_ham + core_ham.T) + field[0] * (0.5 * (dipole + dipole.T))
    ham_b = hamil.astype(jnp.bfloat16)
    part = lax.all_to_all(g2, "pair", split_axis=1, concat_axis=0, tiled=True)
    shape = part.shape
    mixed = jnp.dot(ham_b, part.reshape(shape[0], -1), preferred_element_type=jnp.float32)
    mixed = mixed.astype(jnp.bfloat16).reshape(shape)
    term_i = lax.all_to_all(mixed, "pair", split_axis=0, concat_axis=1, tiled=True)
    wide = lax.all_to_all(g2, "idx", split_axis=1, concat_axis=4, tiled=True)
    lmat = factors.reshape(rank, -1)
    rho_rows = lax.dynamic_slice_in_dim(rho, pair_pos * rows_loc, rows_loc, 1)
    slab_rho = rho[:, :slab, :].astype(jnp.float32)
    rho_local = lax.dynamic_slice_in_dim(rho_rows, idx_pos * kcols, kcols, 2).reshape(2, -1)
    part_x = jnp.dot(lmat, wide.reshape(rows_loc * kcols, -1), preferred_element_type=jnp.float32)
    part_z = lax.dot_general(
        lmat, rho_local, (((1,), (1,)), ((), ())), preferred_element_type=jnp.float32
    )
    total_x, total_z = lax.psum((part_x, part_z), ("pair", "idx"))
    aux = combine(total_x.reshape(rank, 2, slab, width), total_z, slab_rho).astype(jnp.bfloat16)
    ham_cols = jnp.dot(wide.reshape(-1, width), ham_b, preferred_element_type=jnp.float32).reshape(
        wide.shape
    )
    factor_term = lax.dot_general(
        lmat, aux.reshape(rank, -1), (((0,), (0,)), ((), ())), preferred_element_type=jnp.float32
    )
    part_two = (factor_term.reshape(wide.shape) - ham_cols).astype(jnp.bfloat16)
    term_two = lax.all_to_all(part_two, "idx", split_axis=4, concat_axis=1, tiled=True)
    term_k = jnp.einsum(
        "km,imr->ikr", ham_b, g2.reshape(rows_loc, width, -1), preferred_element_type=jnp.float32
    ).reshape(g2.shape)
    values = g2.astype(jnp.float32)
    slab_ham = ham_b[:slab, :slab].astype(jnp.float32)
    term_j = slab_ham[:, 0][None, None, None, :, None] * values
    rate = term_i.astype(jnp.float32) + term_two.astype(jnp.float32) + term_j - term_k
    gam_rows = lax.dynamic_slice_in_dim(damping, pair_pos * rows_loc, rows_loc, 0)
    gam_cols = lax.dynamic_slice_in_dim(damping, idx_pos * cols_loc, cols_loc, 0)
    decay = (
        gam_rows[:, None, None, None]
        + damping[None, :, None, None]
        + damping[:slab][None, None, :, None]
        + gam_cols[None, None, None, :]
    )
    real_next = values[:, :, 0] + step_size * rate[:, :, 1] - step_size * decay * values[:, :, 0]
    imag_next = values[:, :, 1] - step_size * rate[:, :, 0] - step_size * decay * values[:, :, 1]
    return jnp.stack([real_next, imag_next], axis=2).astype(jnp.bfloat16)


def solution(mesh):
    placed = (P("pair", None, None, None, "idx"), P(), P(), P(), P(), P(None, "pair", "idx"), P())
    return jax.shard_map(
        per_device,
        mesh=mesh,
        in_specs=placed,
        out_specs=P("pair", None, None, None, "idx"),
        check_vma=False,
    )
```

profile of v0, /device:TPU:0, one launch (start us, length us, event | category | flops | bytes accessed | tf_op | source)
XLA Modules:
  0.0 1787.3 jit_solution(3607498592157163440)
XLA Ops:
  29.4 188.9 %all_to_all.48 = bf16[64,512,2,1,128]{4,2,3,0,1:T(2,128)(2,1)} all-to-all(bf16[64,512,2,1,128]{4,2,3,0,1:T(2,128)(2,1)S(1)} %copy.83), channel_id=1, replica_groups=mesh['pair'=8,'idx'=4] {'pair'}, dimensions={1} | all-to-all | bytes 33554432 | tf_op jit(solution)/shard_map/all_to_all | solution.py:28
  247.1 360.5 %psum.15 = f32[2048,2]{0,1:T(2,128)S(1)} all-reduce(f32[2048,2]{0,1:T(2,128)S(1)} %fusion.18), channel_id=1, replica_groups=mesh['pair'=8,'idx'=4] {'pair','idx'}, use_global_device_ids=true, to_apply=%region_1.0 | all-reduce | flops 4096 | bytes 32768 | tf_op jit(solution)/shard_map/psum | solution.py:42
  632.4 27.8 %reshape.414 = bf16[512,16384]{1,0:T(8,128)(2,1)} reshape(bf16[8,64,64,2,1,128]{5,3,2,1,0,4:T(2,128)(2,1)} %bitcast.95) | data formatting | bytes 33554432 | tf_op jit(solution)/shard_map/reshape | solution.py:30
  678.4 27.4 %reshape.415 = bf16[512,64,2,1,128]{4,2,1,0,3:T(2,128)(2,1)} reshape(bf16[512,16384]{1,0:T(8,128)(2,1)} %convolution_convert_fusion) | data formatting | bytes 33554432 | tf_op jit(solution)/shard_map/reshape | solution.py:31
  711.8 42.7 %copy.135 = bf16[64,4,128,2,1,128]{5,1,3,2,0,4:T(4,128)(2,1)} copy(bf16[64,4,128,2,1,128]{5,3,0,2,1,4:T(2,128)(2,1)} %bitcast.9) | data formatting | bytes 33554432 | tf_op jit(solution)/shard_map/all_to_all | solution.py:33
  754.5 27.4 %reshape.430 = bf16[8192,1024]{1,0:T(8,128)(2,1)} reshape(bf16[64,128,2,1,4,128]{5,4,2,1,0,3:T(4,128)(2,1)} %bitcast.85) | data formatting | bytes 33554432 | tf_op jit(solution)/shard_map/reshape | solution.py:38
  781.9 45.0 %fusion.2 = f32[2048,1024]{1,0:T(8,128)} fusion(bf16[8192,1024]{1,0:T(8,128)(2,1)} %reshape.430, bf16[256,8,64,128]{3,2,1,0:T(8,128)(2,1)} %bitcast.87), kind=kOutput, calls=%fused_computation.2 | convolution fusion | flops 34359738368 | bytes 58720256 | tf_op jit(solution)/shard_map/dot_general | solution.py:38
  853.5 23.5 %convolution_bitcast_fusion = f32[16384,512]{0,1:T(8,128)} fusion(bf16[512,512]{1,0:T(8,128)(2,1)S(1)} %fusion.23, bf16[2048,8,4,128]{3,2,1,0:T(4,128)(2,1)} %bitcast.86), kind=kOutput, calls=%fused_computation.13 | convolution fusion | flops 8589934592 | bytes 50855936 | tf_op jit(solution)/shard_map/dot_general | solution.py:44
  877.0 33.7 %copy.94 = f32[16384,512]{1,0:T(8,128)} copy(f32[16384,512]{0,1:T(8,128)} %convolution_bitcast_fusion) | data formatting | bytes 67108864 | tf_op jit(solution)/shard_map/dot_general | solution.py:44
  910.6 38.7 %reshape.420 = f32[64,128,2,1,512]{4,2,1,0,3:T(2,128)} reshape(f32[16384,512]{1,0:T(8,128)} %copy.94) | data formatting | bytes 67108864 | tf_op jit(solution)/shard_map/reshape | solution.py:44
  949.3 80.5 %all-reduce.2.cloned.1.call-done = f32[2048,1024]{1,0:T(8,128)} async-done(((f32[2048,1024]{1,0:T(8,128)}), f32[2048,1024]{1,0:T(8,128)}) %all-reduce.2.cloned.1.call-update) | async-done | bytes 8388624 | tf_op jit(solution)/shard_map/psum | solution.py:42
  1029.8 50.2 %fusion.15 = f32[128,8,64,128]{3,1,2,0:T(8,128)} fusion(bf16[256,8,64,128]{3,2,1,0:T(8,128)(2,1)} %bitcast.88, f32[2048,1024]{1,0:T(8,128)} %all-reduce.2.cloned.1.call-done, f32[2048,1024]{1,0:T(8,128)} %copy.93), kind=kOutput, calls=%fused_computation.27 | convolution fusion | flops 34363932672 | bytes 83886080 | tf_op jit(solution)/shard_map/dot_general | solution.py:47
  1080.0 27.8 %copy.106 = f32[128,8,64,128]{3,2,1,0:T(8,128)} copy(f32[128,8,64,128]{3,1,2,0:T(8,128)} %fusion.15) | data formatting | bytes 67108864
  1107.8 34.1 %copy.95 = f32[64,128,2,1,512]{4,1,3,2,0:T(8,128)} copy(f32[64,128,2,1,512]{1,0,4,2,3:T(8,128)} %bitcast.89) | data formatting | bytes 67108864 | tf_op jit(solution)/shard_map/reshape | solution.py:50
  1141.9 28.6 %fusion.4 = bf16[64,128,2,1,512]{4,1,3,2,0:T(8,128)(2,1)} fusion(f32[64,128,2,1,512]{4,1,3,2,0:T(8,128)} %copy.95, f32[64,128,2,1,512]{4,2,1,0,3:T(2,128)} %reshape.420), kind=kLoop, calls=%fused_computation.7 | loop fusion | flops 16777216 | bytes 83886080 | tf_op jit(solution)/shard_map/convert_element_type | solution.py:50
  1170.6 23.2 %copy.97 = bf16[64,128,2,1,512]{1,0,3,2,4:T(8,128)(2,1)} copy(bf16[64,128,2,1,512]{4,1,3,2,0:T(8,128)(2,1)} %fusion.4) | data formatting | bytes 33554432 | tf_op jit(solution)/shard_map/convert_element_type | solution.py:50
  1200.8 40.8 %copy.103 = bf16[64,512,2,1,128]{1,4,2,0,3:T(8,128)(2,1)} copy(bf16[64,512,2,1,128]{4,2,3,1,0:T(2,128)(2,1)} %param.7) | data formatting | bytes 33554432 | tf_op jit(solution)/shard_map/reshape | solution.py:53
  1282.3 48.5 %copy.100 = f32[64,512,2,1,128]{4,2,3,1,0:T(2,128)} copy(f32[64,512,2,1,128]{1,4,2,0,3:T(8,128)} %bitcast.84) | data formatting | bytes 67108864 | tf_op jit(solution)/shard_map/reshape | solution.py:54
  1349.8 23.0 %copy.86 = f32[64,8,64,2,1,128]{5,3,2,1,0,4:T(2,128)} copy(f32[64,8,64,2,1,128]{5,3,2,0,1,4:T(2,128)} %convert_bitcast_fusion.1) | data formatting | bytes 67108864 | tf_op jit(solution)/shard_map/convert_element_type | solution.py:58
  1372.8 190.9 %all-to-all-done.3 = bf16[64,128,2,1,512]{1,0,3,2,4:T(8,128)(2,1)} async-done(((bf16[64,128,2,1,512]{1,0,3,2,4:T(8,128)(2,1)}), bf16[64,128,2,1,512]{1,0,3,2,4:T(8,128)(2,1)}, u32[]{:S(2)}, u32[]{:S(2)}) %all-to-all-start.3) | async-done | bytes 16777248 | tf_op jit(solution)/shard_map/all_to_all | solution.py:51
  1582.3 38.4 %copy.98 = f32[64,4,128,2,1,128]{5,3,2,1,0,4:T(2,128)} copy(f32[64,4,128,2,1,128]{2,0,3,5,1,4:T(8,128)} %convert_bitcast_fusion) | data formatting | bytes 67108864 | tf_op jit(solution)/shard_map/convert_element_type | solution.py:58
  1620.7 47.8 %add_subtract_fusion = f32[64,512,2,1,128]{4,2,3,1,0:T(2,128)} fusion(f32[64,512,2,1,128]{4,2,3,1,0:T(2,128)} %copy.100, f32[64,512,2,1,128]{4,2,3,1,0:T(2,128)} %bitcast.90, f32[64,512,2,1,128]{4,2,3,1,0:T(2,128)} %bitcast.91, f32[]{:T(128)S(6)} %convert.17, bf16[64,512,2,1,128]{4,2,3,1,0:T(2,128)(2,1)} %param.7), kind=kLoop, calls=%fused_computation.10 | loop fusion | flops 41943040 | bytes 150994944 | tf_op jit(solution)/shard_map/sub | solution.py:58
  1668.5 70.8 %fusion.14 = (bf16[64,512,1,1,128]{4,2,3,1,0:T(2,128)(2,1)S(1)}, bf16[64,512,1,1,128]{4,2,3,1,0:T(2,128)(2,1)}) fusion(f32[64,512,2,1,128]{4,2,3,1,0:T(2,128)} %add_subtract_fusion, f32[64,512,2,1,128]{4,2,3,1,0:T(2,128)} %convert_element_type.79, f32[128]{0:T(128)S(1)} %copy-done.6, f32[64,512]{1,0:T(8,128)S(1)} %add_add_fusion), kind=kLoop, calls=%fused_computation.26 | loop fusion | flops 37748736 | bytes 84017664 | tf_op jit(solution)/shard_map/convert.7
  1739.3 40.7 %pad_maximum_fusion = bf16[64,512,2,1,128]{4,2,3,1,0:T(2,128)(2,1)} fusion(bf16[64,512,1,1,128]{4,2,3,1,0:T(2,128)(2,1)} %get-tuple-element.6, bf16[64,512,1,1,128]{4,2,3,1,0:T(2,128)(2,1)S(1)} %get-tuple-element.5), kind=kLoop, calls=%fused_computation.23 | loop fusion | flops 33554432 | bytes 33554432 | tf_op jit(solution)/shard_map/stack | solution.py:69
  (45 shorter events, 211.2 us)
Async XLA Ops:
  23.7 5.7 copy-start
  218.4 7.2 copy-start.4
  218.4 8.6 copy-start.3
  218.4 487.5 %all-to-all-start.2 = ((bf16[64,512,2,1,128]{4,2,3,0,1:T(2,128)(2,1)}), bf16[64,512,2,1,128]{4,2,3,0,1:T(2,128)(2,1)}, u32[]{:S(2)}, u32[]{:S(2)}) async-start(bf16[64,512,2,1,128]{4,2,3,0,1:T(2,128)(2,1)} %copy-done), calls=%async_computation.2 | async-start | bytes 33554432 | tf_op jit(solution)/shard_map/all_to_all | solution.py:33
  610.4 243.1 %copy-start.1 = (bf16[512,512]{1,0:T(8,128)(2,1)}, bf16[512,512]{1,0:T(8,128)(2,1)S(1)}, u32[]{:S(2)}) copy-start(bf16[512,512]{1,0:T(8,128)(2,1)S(1)} %fusion.23) | copy-start | bytes 1572868
  705.8 487.9 %all-to-all-start.1 = ((bf16[512,64,2,1,128]{4,2,1,3,0:T(2,128)(2,1)}), bf16[512,64,2,1,128]{4,2,1,3,0:T(2,128)(2,1)}, u32[]{:S(2)}, u32[]{:S(2)}) async-start(bf16[512,64,2,1,128]{4,2,1,3,0:T(2,128)(2,1)} %bitcast.94), calls=%async_computation.1 | async-start | bytes 33554432 | tf_op jit(solution)/shard_map/all_to_all | solution.py:32
  711.6 318.2 %all-reduce.2.cloned.1.call-start = ((), (), s32[]{:S(2)}) async-start(), calls=%async_computation.4 | async-start | bytes 16777216 | tf_op jit(solution)/shard_map/psum | solution.py:42
  1193.7 369.9 %all-to-all-start.3 = ((bf16[64,128,2,1,512]{1,0,3,2,4:T(8,128)(2,1)}), bf16[64,128,2,1,512]{1,0,3,2,4:T(8,128)(2,1)}, u32[]{:S(2)}, u32[]{:S(2)}) async-start(bf16[64,128,2,1,512]{1,0,3,2,4:T(8,128)(2,1)} %copy.97), calls=%async_computation.3 | async-start | bytes 33554432 | tf_op jit(solution)/shard_map/all_to_all | solution.py:51
  1200.8 40.9 %copy-start.2 = (bf16[512,512]{1,0:T(8,128)(2,1)S(1)}, bf16[512,512]{1,0:T(8,128)(2,1)}, u32[]{:S(2)}) copy-start(bf16[512,512]{1,0:T(8,128)(2,1)} %copy-done.1) | copy-start | bytes 1572868
  1200.8 41.4 %copy-start.5 = (f32[512]{0:T(512)S(1)}, f32[512]{0:T(512)}, u32[]{:S(2)}) copy-start(f32[512]{0:T(512)} %param.13) | copy-start | bytes 6148
  1620.7 47.8 %copy-start.6 = (f32[128]{0:T(128)S(1)}, f32[128]{0:T(128)}, u32[]{:S(2)}) copy-start(f32[128]{0:T(128)} %dynamic_slice.13) | copy-start | bytes 1540
Sparse Core Ops, SparseCore 0:
  827.1 202.6 all-reduce.1
where the time goes:
time: 1800 us; the launch traced here: 1790 us
  blocking collectives  549 us (30%)
  local copies, waits for them, and re-layouts  498 us (28%)
  waiting for transfers between devices  271 us (15%)
  other arithmetic  257 us (14%)
  matrix products  175 us (10%)
  starting transfers between devices  20.2 us (1%)
    psum x1, blocking collectives, per_device(): total_x, total_z = lax.psum((part_x, part_z), ('pair', 'idx'))  360 us
    all_to_all x1, waiting for transfers between devices, per_device(): lax.all_to_all(part_two, 'idx', split_axis=4, concat_axis=1, tiled=True)  191 us
    all_to_all x1, blocking collectives, per_device(): part = lax.all_to_all(g2, 'pair', split_axis=1, concat_axis=0, tiled=True)  189 us
    psum x1, waiting for transfers between devices, per_device(): total_x, total_z = lax.psum((part_x, part_z), ('pair', 'idx'))  80.5 us
    another operation x1, other arithmetic  70.8 us
    unnamed x18, local copies, waits for them, and re-layouts  53.4 us
    dot_general x1, matrix products, per_device(): lax.dot_general(lmat, aux.reshape(rank, -1), (((0,), (0,)), ((), ())), pr...  50.2 us
    reshape x1, local copies, waits for them, and re-layouts, per_device(): term_k = jnp.einsum('km,imr->ikr', ham_b, g2.reshape(rows_loc, width, -1)...  48.5 us
  transfers between devices with their start and end apart: 4, of which 2 were waited for; matrix products, arithmetic and copies ran while one was open for 39% of the time, Pallas kernels for 0%

commit v1 on v0

--- a/solution.py
+++ b/solution.py
@@ -48,7 +48,18 @@
         lmat, aux.reshape(rank, -1), (((0,), (0,)), ((), ())), preferred_element_type=jnp.float32
     )
     part_two = (factor_term.reshape(wide.shape) - ham_cols).astype(jnp.bfloat16)
-    term_two = lax.all_to_all(part_two, "idx", split_axis=4, concat_axis=1, tiled=True)
+    block_next, r1 = (jax.lax.axis_size("idx"), jax.lax.axis_index("idx"))
+    after = part_two.shape[4] // block_next
+    x_now = list(part_two.shape)
+    x_now[4] = after
+    local_out = x_now[1]
+    x_now[1] = local_out * block_next
+    term_two = jnp.zeros(x_now, part_two.dtype)
+    for to_i in range(block_next):
+        high = lax.dynamic_slice_in_dim(part_two, (r1 ^ to_i) * after, after, axis=4)
+        if to_i:
+            high = jax.lax.ppermute(high, "idx", tuple(((j, j ^ to_i) for j in range(block_next))))
+        term_two = lax.dynamic_update_slice_in_dim(term_two, high, (r1 ^ to_i) * local_out, axis=1)
     term_k = jnp.einsum(
         "km,imr->ikr", ham_b, g2.reshape(rows_loc, width, -1), preferred_element_type=jnp.float32
     ).reshape(g2.shape)

time: 1800 us -> 1880 us (1.044)
  the two profiles are of different devices: /device:TPU:0 before, /device:TPU:8 now
where the time goes in v1:
time: 1880 us; the launch traced here: 1860 us
  local copies, waits for them, and re-layouts  509 us (27%)
  blocking collectives  490 us (26%)
  waiting for transfers between devices  439 us (23%)
  other arithmetic  220 us (12%)
  matrix products  175 us (9%)
    psum x1, blocking collectives, per_device(): total_x, total_z = lax.psum((part_x, part_z), ('pair', 'idx'))  302 us
    ppermute x3, waiting for transfers between devices, per_device(): jax.lax.ppermute(high, 'idx', tuple(((j, j ^ to_i) for j in range(block_n...  278 us
    all_to_all x1, blocking collectives, per_device(): part = lax.all_to_all(g2, 'pair', split_axis=1, concat_axis=0, tiled=True)  188 us
    psum x1, waiting for transfers between devices, per_device(): total_x, total_z = lax.psum((part_x, part_z), ('pair', 'idx'))  161 us
    another operation x1, other arithmetic  70.8 us
    unnamed x18, local copies, waits for them, and re-layouts  58.9 us
    dot_general x1, matrix products, per_device(): lax.dot_general(lmat, aux.reshape(rank, -1), (((0,), (0,)), ((), ())), pr...  50.2 us
    reshape x1, local copies, waits for them, and re-layouts, per_device(): term_k = jnp.einsum('km,imr->ikr', ham_b, g2.reshape(rows_loc, width, -1)...  48.6 us
  transfers between devices with their start and end apart: 6, of which 4 were waited for; matrix products, arithmetic and copies ran while one was open for 32% of the time, Pallas kernels for 0%

profile of v1, /device:TPU:8, one launch (start us, length us, event | category | flops | bytes accessed | tf_op | source)
XLA Modules:
  0.0 1864.7 jit_solution(3805267822345459376)
XLA Ops:
  29.4 187.7 %all_to_all.39 = bf16[64,512,2,1,128]{4,2,3,0,1:T(2,128)(2,1)} all-to-all(bf16[64,512,2,1,128]{4,2,3,0,1:T(2,128)(2,1)S(1)} %copy.73), channel_id=1, replica_groups=mesh['pair'=8,'idx'=4] {'pair'}, dimensions={1} | all-to-all | bytes 33554432 | tf_op jit(solution)/shard_map/all_to_all | solution.py:28
  224.3 40.8 %copy.94 = bf16[64,512,2,1,128]{1,4,2,0,3:T(8,128)(2,1)} copy(bf16[64,512,2,1,128]{4,2,3,1,0:T(2,128)(2,1)} %param.7) | data formatting | bytes 33554432 | tf_op jit(solution)/shard_map/reshape | solution.py:64
  301.9 302.4 %psum.15 = f32[2048,2]{0,1:T(2,128)S(1)} all-reduce(f32[2048,2]{0,1:T(2,128)S(1)} %fusion.17), channel_id=1, replica_groups=mesh['pair'=8,'idx'=4] {'pair','idx'}, use_global_device_ids=true, to_apply=%region_1.0 | all-reduce | flops 4096 | bytes 32768 | tf_op jit(solution)/shard_map/psum | solution.py:42
  634.4 21.2 %fusion.24 = f32[512,64,256]{0,2,1:T(8,128)} fusion(bf16[64,512,256]{1,2,0:T(8,128)(2,1)} %bitcast.94, bf16[512,512]{1,0:T(8,128)(2,1)S(1)} %fusion.22), kind=kOutput, calls=%fused_computation.41 | convolution fusion | flops 8589934592 | bytes 50855936 | tf_op jit(solution)/shard_map/km,imr->ikr/dot_general | solution.py:63
  655.7 48.6 %copy.91 = f32[64,512,2,1,128]{4,2,3,1,0:T(2,128)} copy(f32[64,512,2,1,128]{1,4,2,0,3:T(8,128)} %bitcast.87) | data formatting | bytes 67108864 | tf_op jit(solution)/shard_map/reshape | solution.py:65
  724.4 27.7 %reshape.394 = bf16[512,16384]{1,0:T(8,128)(2,1)} reshape(bf16[8,64,64,2,1,128]{5,3,2,1,0,4:T(2,128)(2,1)} %bitcast.97) | data formatting | bytes 33554432 | tf_op jit(solution)/shard_map/reshape | solution.py:30
  752.2 42.7 %copy.123 = bf16[64,4,128,2,1,128]{5,1,3,2,0,4:T(4,128)(2,1)} copy(bf16[64,4,128,2,1,128]{5,3,0,2,1,4:T(2,128)(2,1)} %bitcast.9) | data formatting | bytes 33554432 | tf_op jit(solution)/shard_map/all_to_all | solution.py:33
  794.9 27.8 %reshape.408 = bf16[8192,1024]{1,0:T(8,128)(2,1)} reshape(bf16[64,128,2,1,4,128]{5,4,2,1,0,3:T(4,128)(2,1)} %bitcast.88) | data formatting | bytes 33554432 | tf_op jit(solution)/shard_map/reshape | solution.py:38
  822.6 44.8 %fusion.2 = f32[2048,1024]{1,0:T(8,128)} fusion(bf16[8192,1024]{1,0:T(8,128)(2,1)} %reshape.408, bf16[256,8,64,128]{3,2,1,0:T(8,128)(2,1)} %bitcast.90), kind=kOutput, calls=%fused_computation.2 | convolution fusion | flops 34359738368 | bytes 58720256 | tf_op jit(solution)/shard_map/dot_general | solution.py:38
  885.7 27.7 %reshape.395 = bf16[512,64,2,1,128]{4,2,1,0,3:T(2,128)(2,1)} reshape(bf16[512,16384]{1,0:T(8,128)(2,1)} %convolution_convert_fusion) | data formatting | bytes 33554432 | tf_op jit(solution)/shard_map/reshape | solution.py:31
  919.3 23.2 %convolution_bitcast_fusion = f32[16384,512]{0,1:T(8,128)} fusion(bf16[512,512]{1,0:T(8,128)(2,1)S(1)} %fusion.22, bf16[2048,8,4,128]{3,2,1,0:T(4,128)(2,1)} %bitcast.89), kind=kOutput, calls=%fused_computation.11 | convolution fusion | flops 8589934592 | bytes 50855936 | tf_op jit(solution)/shard_map/dot_general | solution.py:44
  942.5 33.4 %copy.84 = f32[16384,512]{1,0:T(8,128)} copy(f32[16384,512]{0,1:T(8,128)} %convolution_bitcast_fusion) | data formatting | bytes 67108864 | tf_op jit(solution)/shard_map/dot_general | solution.py:44
  975.9 39.1 %reshape.400 = f32[64,128,2,1,512]{4,2,1,0,3:T(2,128)} reshape(f32[16384,512]{1,0:T(8,128)} %copy.84) | data formatting | bytes 67108864 | tf_op jit(solution)/shard_map/reshape | solution.py:44
  1015.0 160.8 %all-reduce.2.cloned.1.call-done = f32[2048,1024]{1,0:T(8,128)} async-done(((f32[2048,1024]{1,0:T(8,128)}), f32[2048,1024]{1,0:T(8,128)}) %all-reduce.2.cloned.1.call-update) | async-done | bytes 8388624 | tf_op jit(solution)/shard_map/psum | solution.py:42
  1175.8 50.2 %fusion.14 = f32[128,8,64,128]{3,1,2,0:T(8,128)} fusion(bf16[256,8,64,128]{3,2,1,0:T(8,128)(2,1)} %bitcast.91, f32[2048,1024]{1,0:T(8,128)} %all-reduce.2.cloned.1.call-done, f32[2048,1024]{1,0:T(8,128)} %copy.83), kind=kOutput, calls=%fused_computation.25 | convolution fusion | flops 34363932672 | bytes 83886080 | tf_op jit(solution)/shard_map/dot_general | solution.py:47
  1226.0 27.5 %copy.97 = f32[128,8,64,128]{3,2,1,0:T(8,128)} copy(f32[128,8,64,128]{3,1,2,0:T(8,128)} %fusion.14) | data formatting | bytes 67108864
  1253.5 38.6 %copy.85 = f32[64,128,2,1,512]{4,2,1,0,3:T(2,128)} copy(f32[64,128,2,1,512]{1,0,4,2,3:T(8,128)} %bitcast.92) | data formatting | bytes 67108864 | tf_op jit(solution)/shard_map/reshape | solution.py:50
  1371.0 23.0 %copy.76 = f32[64,8,64,2,1,128]{5,3,2,1,0,4:T(2,128)} copy(f32[64,8,64,2,1,128]{5,3,2,0,1,4:T(2,128)} %convert_bitcast_fusion) | data formatting | bytes 67108864 | tf_op jit(solution)/shard_map/convert_element_type | solution.py:69
  1393.9 115.0 %collective-permute-done = bf16[64,128,2,1,128]{4,2,1,0,3:T(2,128)(2,1)} collective-permute-done((bf16[64,128,2,1,128]{4,2,1,0,3:T(2,128)(2,1)}, bf16[64,128,2,1,128]{4,2,1,0,3:T(2,128)(2,1)}, u32[]{:S(2)}, u32[]{:S(2)}) %collective-permute-start) | collective-permute-done | bytes 4194336 | tf_op jit(solution)/shard_map/ppermute | solution.py:61
  1519.3 84.1 %collective-permute-done.1 = bf16[64,128,2,1,128]{4,2,1,0,3:T(2,128)(2,1)} collective-permute-done((bf16[64,128,2,1,128]{4,2,1,0,3:T(2,128)(2,1)}, bf16[64,128,2,1,128]{4,2,1,0,3:T(2,128)(2,1)}, u32[]{:S(2)}, u32[]{:S(2)}) %collective-permute-start.1) | collective-permute-done | bytes 4194336 | tf_op jit(solution)/shard_map/ppermute | solution.py:61
  1613.8 78.9 %collective-permute-done.2 = bf16[64,128,2,1,128]{4,2,1,0,3:T(2,128)(2,1)} collective-permute-done((bf16[64,128,2,1,128]{4,2,1,0,3:T(2,128)(2,1)}, bf16[64,128,2,1,128]{4,2,1,0,3:T(2,128)(2,1)}, u32[]{:S(2)}, u32[]{:S(2)}) %collective-permute-start.2) | collective-permute-done | bytes 4194336 | tf_op jit(solution)/shard_map/ppermute | solution.py:61
  1703.1 43.0 %add_subtract_fusion = f32[64,512,2,1,128]{4,2,3,1,0:T(2,128)} fusion(f32[64,512,2,1,128]{4,2,3,1,0:T(2,128)} %copy.91, f32[64,512,2,1,128]{4,2,3,1,0:T(2,128)} %bitcast.93, bf16[64,512,2,1,128]{4,2,3,1,0:T(2,128)(2,1)} %bitcast_dynamic-update-slice_fusion, f32[]{:T(128)S(6)} %convert.13, bf16[64,512,2,1,128]{4,2,3,1,0:T(2,128)(2,1)} %param.7), kind=kLoop, calls=%fused_computation.7 | loop fusion | flops 50331648 | bytes 134217728 | tf_op jit(solution)/shard_map/sub | solution.py:69
  1746.2 70.8 %fusion.13 = (bf16[64,512,1,1,128]{4,2,3,1,0:T(2,128)(2,1)S(1)}, bf16[64,512,1,1,128]{4,2,3,1,0:T(2,128)(2,1)}) fusion(f32[64,512,2,1,128]{4,2,3,1,0:T(2,128)} %add_subtract_fusion, f32[64,512,2,1,128]{4,2,3,1,0:T(2,128)} %convert_element_type.62, f32[128]{0:T(128)S(1)} %copy-done.6, f32[64,512]{1,0:T(8,128)S(1)} %copy-done.4), kind=kLoop, calls=%fused_computation.24 | loop fusion | flops 37748736 | bytes 84017664 | tf_op jit(solution)/shard_map/convert.4
  1816.9 40.7 %pad_maximum_fusion = bf16[64,512,2,1,128]{4,2,3,1,0:T(2,128)(2,1)} fusion(bf16[64,512,1,1,128]{4,2,3,1,0:T(2,128)(2,1)} %get-tuple-element.6, bf16[64,512,1,1,128]{4,2,3,1,0:T(2,128)(2,1)S(1)} %get-tuple-element.5), kind=kLoop, calls=%fused_computation.21 | loop fusion | flops 33554432 | bytes 33554432 | tf_op jit(solution)/shard_map/stack | solution.py:80
  (52 shorter events, 250.0 us)
Async XLA Ops:
  23.7 5.7 copy-start
  217.1 535.1 %all-to-all-start.2 = ((bf16[64,512,2,1,128]{4,2,3,0,1:T(2,128)(2,1)}), bf16[64,512,2,1,128]{4,2,3,0,1:T(2,128)(2,1)}, u32[]{:S(2)}, u32[]{:S(2)}) async-start(bf16[64,512,2,1,128]{4,2,3,0,1:T(2,128)(2,1)} %copy-done), calls=%async_computation.2 | async-start | bytes 33554432 | tf_op jit(solution)/shard_map/all_to_all | solution.py:33
  224.3 951.5 %all-reduce.2.cloned.1.call-start = ((), (), s32[]{:S(2)}) async-start(), calls=%async_computation.3 | async-start | bytes 16777216 | tf_op jit(solution)/shard_map/psum | solution.py:42
  265.0 17.5 copy-start.5
  610.3 18.2 copy-start.3
  610.3 19.5 %copy-start.2 = (f32[512,512]{1,0:T(8,128)S(1)}, f32[512,512]{1,0:T(8,128)}, u32[]{:S(2)}) copy-start(f32[512,512]{1,0:T(8,128)} %param.9) | copy-start | bytes 3145732
  913.4 440.0 %all-to-all-start.1 = ((bf16[512,64,2,1,128]{4,2,1,3,0:T(2,128)(2,1)}), bf16[512,64,2,1,128]{4,2,1,3,0:T(2,128)(2,1)}, u32[]{:S(2)}, u32[]{:S(2)}) async-start(bf16[512,64,2,1,128]{4,2,1,3,0:T(2,128)(2,1)} %bitcast.96), calls=%async_computation.1 | async-start | bytes 33554432 | tf_op jit(solution)/shard_map/all_to_all | solution.py:32
  1313.2 5.8 copy-start.1
  1329.4 179.5 %collective-permute-start = (bf16[64,128,2,1,128]{4,2,1,0,3:T(2,128)(2,1)}, bf16[64,128,2,1,128]{4,2,1,0,3:T(2,128)(2,1)}, u32[]{:S(2)}, u32[]{:S(2)}) collective-permute-start(bf16[64,128,2,1,128]{4,2,1,0,3:T(2,128)(2,1)} %get-tuple-element.9), channel_id=1, source_target_pairs={{0,1},{1,0},{2,3},{3,2},{4,5},{5,4},{6,7},{7,6},{8,9},{9,8},{10,11... | collective-permute-start | bytes 12582920 | tf_op jit(solution)/shard_map/ppermute | solution.py:61
  1330.0 273.4 %collective-permute-start.1 = (bf16[64,128,2,1,128]{4,2,1,0,3:T(2,128)(2,1)}, bf16[64,128,2,1,128]{4,2,1,0,3:T(2,128)(2,1)}, u32[]{:S(2)}, u32[]{:S(2)}) collective-permute-start(bf16[64,128,2,1,128]{4,2,1,0,3:T(2,128)(2,1)} %get-tuple-element.8), channel_id=1, source_target_pairs={{0,2},{1,3},{2,0},{3,1},{4,6},{5,7},{6,4},{7,5},{8,10},{9,11},{10,... | collective-permute-start | bytes 12582920 | tf_op jit(solution)/shard_map/ppermute | solution.py:61
  1332.4 360.3 %collective-permute-start.2 = (bf16[64,128,2,1,128]{4,2,1,0,3:T(2,128)(2,1)}, bf16[64,128,2,1,128]{4,2,1,0,3:T(2,128)(2,1)}, u32[]{:S(2)}, u32[]{:S(2)}) collective-permute-start(bf16[64,128,2,1,128]{4,2,1,0,3:T(2,128)(2,1)} %get-tuple-element.7), channel_id=1, source_target_pairs={{0,3},{1,2},{2,1},{3,0},{4,7},{5,6},{6,5},{7,4},{8,11},{9,10},{10,... | collective-permute-start | bytes 12582920 | tf_op jit(solution)/shard_map/ppermute | solution.py:61
  1703.1 43.0 %copy-start.4 = (f32[64,512]{1,0:T(8,128)S(1)}, f32[64,512]{1,0:T(8,128)}, u32[]{:S(2)}) copy-start(f32[64,512]{1,0:T(8,128)} %add_add_fusion) | copy-start | bytes 393220
  1703.1 43.0 %copy-start.6 = (f32[128]{0:T(128)S(1)}, f32[128]{0:T(128)}, u32[]{:S(2)}) copy-start(f32[128]{0:T(128)} %dynamic_slice.29) | copy-start | bytes 1540
Sparse Core Ops, SparseCore 0:
  867.6 308.2 all-reduce.1
